TPU v7x, 512 devices: a whole 4x8x8 slice. The times are simulated.
512 devices in a mesh: line: 64 (over z, x, core), span: 8 (over y).
Axes of the slice: x: 4, y: 8, z: 8, core: 2. Of those that a mesh axis runs over, the one named last changes fastest.
Arguments:
- jacobian: bfloat16 [5, 5, 8, 4096, 128], P(None, None, 'span', 'line'), may hold values from -1 to 1
- state: float32 [5, 8, 4096, 128], P(None, 'span', 'line'), may hold values from -6 to 6
- metric: float32 [8, 4096, 128], P('span', 'line'), may hold values from 0.5 to 1.5
- dissipation: float32 [8, 4096, 128], P('span', 'line'), may hold values from 2 to 10
- time_term: float32 [8, 4096, 128], P('span', 'line'), may hold values from 0.0001 to 0.0005
Outputs:
- update: float32 [5, 8, 4096, 128], P(None, 'span', 'line')
All inputs are finite; a program needn't handle non-finite values.
Results may differ from a plain program's by a relative error of at most 0.0003.
Values sent between devices are 32-bit elements; how exact they have to be, the bound alone decides.
A program may use at most 64 MiB of HBM per device.

v0:
```python
import jax
import jax.numpy as jnp
from jax import lax
from jax.experimental import pallas as pl
from jax.experimental.pallas import tpu as pltpu
from jax.sharding import PartitionSpec as P

MESH = pl.DeviceIdType.MESH
f32 = jnp.float32
span_weight = 0.25
NV = 5
GROUP = 8
WIDE = 16
PACKS = 14
PAIRS = [(i, j) for i in range(NV) for j in range(i, NV)]
SYM = [[PAIRS.index((min(i, j), max(i, j))) for j in range(NV)] for i in range(NV)]
NSYM = len(PAIRS)


def roll(x, shift, axis):
    return pltpu.roll(x, shift, axis)


def mm(left, right):
    out = []
    for i in range(NV):
        acc = left[i][0][None] * right[0]
        for k in range(1, NV):
            acc = acc + left[i][k][None] * right[k]
        out.append(acc)
    return out


def inverse(m):
    m = [list(row) for row in m]
    for p in range(NV):
        r = 1.0 / m[p][p]
        for j in range(NV):
            if j != p:
                m[p][j] = m[p][j] * r
        for i in range(NV):
            if i != p:
                f = m[i][p]
                for j in range(NV):
                    if j != p:
                        m[i][j] = m[i][j] - f * m[p][j]
                m[i][p] = -(f * r)
        m[p][p] = r
    return m


def tree_up(seg, la_ref, fb_ref, axis, size, base):
    def body(level, carry):
        back = size - lax.shift_left(jnp.int32(base), level)
        fa = [seg[0, i] for i in range(NV)]
        la = [seg[1, i] for i in range(NV)]
        fb = [roll(x, back, axis) for x in fa]
        lb = [roll(x, back, axis) for x in la]
        t = mm([[la[i][NV + k] for k in range(NV)] for i in range(NV)], fb)
        eye = [[(1.0 if i == k else 0.0) - t[i][k] for k in range(NV)] for i in range(NV)]
        x = inverse(eye)
        q = [
            jnp.concatenate(
                [la[i][0:NV], -t[i][NV : 2 * NV], la[i][2 * NV :] - t[i][2 * NV :]], axis=0
            )
            for i in range(NV)
        ]
        ela = mm(x, q)
        r = mm([[fb[i][k] for k in range(NV)] for i in range(NV)], ela)
        efb = [
            jnp.concatenate([-r[i][0:NV], fb[i][NV:] - r[i][NV:]], axis=0) for i in range(NV)
        ]
        s = mm([[fa[i][NV + k] for k in range(NV)] for i in range(NV)], efb)
        y = mm([[lb[i][k] for k in range(NV)] for i in range(NV)], ela)
        for i in range(NV):
            la_ref[level, i] = ela[i]
            fb_ref[level, i] = efb[i]
            seg[0, i, 0:NV] = fa[i][0:NV] - s[i][0:NV]
            seg[0, i, NV : 2 * NV] = -s[i][NV : 2 * NV]
            seg[0, i, 2 * NV :] = fa[i][2 * NV :] - s[i][2 * NV :]
            seg[1, i, 0:NV] = -y[i][0:NV]
            seg[1, i, NV:] = lb[i][NV:] - y[i][NV:]
        return carry

    lax.fori_loop(0, 3, body, 0)


def tree_down(p, n, la_ref, fb_ref, axis, base, pos):
    for level in (2, 1, 0):
        shift = base << level
        pn = jnp.concatenate([p, n], axis=0)
        la = []
        fb = []
        for i in range(NV):
            la.append(
                la_ref[level, i, 2 * NV :]
                - jnp.sum(la_ref[level, i, 0 : 2 * NV] * pn, axis=0, keepdims=True)
            )
            fb.append(
                fb_ref[level, i, 2 * NV :]
                - jnp.sum(fb_ref[level, i, 0 : 2 * NV] * pn, axis=0, keepdims=True)
            )
        la = jnp.concatenate(la, axis=0)
        fb = jnp.concatenate(fb, axis=0)
        second = (pos & shift) != 0
        p, n = (
            jnp.where(second, roll(la, shift, axis), p),
            jnp.where(second, roll(n, shift, axis), fb),
        )
    return p, n


def swap_blocks(x):
    sub = lax.broadcasted_iota(jnp.int32, x.shape, 1)
    lane = lax.broadcasted_iota(jnp.int32, x.shape, 2)
    for bit in range(3):
        j = lax.shift_right_logical(sub, bit) & 1
        k = lax.shift_right_logical(lane, 4 + bit) & 1
        s = 1 << bit
        w = WIDE << bit
        up = roll(roll(x, GROUP - s, 1), w, 2)
        down = roll(roll(x, s, 1), 128 - w, 2)
        x = jnp.where(j == k, x, jnp.where(j == 0, up, down))
    return x


def kernel(
    jac_ref, state_ref, metric_ref, diss_ref, time_ref, out_ref,
    sym_ref, flux_ref, fst, dst, xst, ls, us, fs,
    rim_out, rim_in, span_in,
    wc, pinv, hg, es,
    seg1, la1, fb1, seg2, la2, fb2, seg3, la3, fb3,
    tmp, a_out, a_in, b_out, b_in, c_out, c_in,
    span_sem, rim_sem, a_sem, b_sem, c_sem,
):
    line = lax.axis_index("line")
    span = lax.axis_index("span")
    n_line = lax.axis_size("line")
    n_span = lax.axis_size("span")
    plane = line // GROUP
    member = line % GROUP
    line_next = lax.rem(line + 1, n_line)
    line_prev = lax.rem(line + n_line - 1, n_line)
    span_next = lax.rem(span + 1, n_span)
    span_prev = lax.rem(span + n_span - 1, n_span)
    members = [plane * GROUP + lax.rem(member + o, GROUP) for o in range(1, GROUP)]
    planes = [lax.rem(plane + o, GROUP) * GROUP + member for o in range(1, GROUP)]

    peers = [(line, span_next), (line, span_prev), (line_next, span), (line_prev, span)]
    peers += [(x, span) for x in members] + [(x, span) for x in planes]
    barrier = pltpu.get_barrier_semaphore()
    for peer in peers:
        pl.semaphore_signal(barrier, inc=1, device_id=peer, device_id_type=MESH)

    metric = metric_ref[...]
    for q, (i, j) in enumerate(PAIRS):
        if i == j:
            value = jac_ref[i, i].astype(f32)
        else:
            value = 0.5 * (jac_ref[i, j].astype(f32) + jac_ref[j, i].astype(f32))
        sym_ref[q] = metric * value
    for i in range(NV):
        acc = sym_ref[SYM[i][0]] * state_ref[0]
        for k in range(1, NV):
            acc = acc + sym_ref[SYM[i][k]] * state_ref[k]
        flux_ref[i] = acc
    points = metric.shape[0]
    for side, row in ((0, points - 1), (1, 0)):
        for q in range(NSYM):
            rim_out[side, q : q + 1, :] = sym_ref[q, row : row + 1, :]
        for i in range(NV):
            rim_out[side, NSYM + i : NSYM + i + 1, :] = flux_ref[i, row : row + 1, :]
        rim_out[side, NSYM + NV : NSYM + NV + 1, :] = diss_ref[row : row + 1, :]
        rim_out[side, NSYM + NV + 1 :, :] = jnp.zeros((24 - NSYM - NV - 1, 128), f32)

    pl.semaphore_wait(barrier, len(peers))

    copies_rim = []
    for side, target in ((0, line_next), (1, line_prev)):
        copies_rim.append(
            pltpu.make_async_remote_copy(
                src_ref=rim_out.at[side], dst_ref=rim_in.at[side],
                send_sem=rim_sem.at[0, side], recv_sem=rim_sem.at[1, side],
                device_id=(target, span), device_id_type=MESH,
            )
        )
        copies_rim[-1].start()
    copies_span = []
    for side, target in ((0, span_next), (1, span_prev)):
        copies_span.append(
            pltpu.make_async_remote_copy(
                src_ref=state_ref, dst_ref=span_in.at[side],
                send_sem=span_sem.at[0, side], recv_sem=span_sem.at[1, side],
                device_id=(line, target), device_id_type=MESH,
            )
        )
        copies_span[-1].start()

    for t in range(GROUP):
        fst[t + 1] = sym_ref[:, pl.ds(t, GROUP, stride=GROUP), :]
        xst[t + 1] = flux_ref[:, pl.ds(t, GROUP, stride=GROUP), :]
        dst[t + 1] = diss_ref[pl.ds(t, GROUP, stride=GROUP), :]
    sub3 = lax.broadcasted_iota(jnp.int32, (1, GROUP, 128), 1)
    sub2 = lax.broadcasted_iota(jnp.int32, (GROUP, 128), 0)
    for c in copies_rim:
        c.wait()
    first_device = line == 0
    last_device = line == n_line - 1
    for side, at, source, turn, edge, outside in (
        (0, 0, GROUP, 1, 0, first_device),
        (1, GROUP + 1, 1, GROUP - 1, GROUP - 1, last_device),
    ):
        rim = jnp.where(outside, 0.0, rim_in[side])
        for q in range(NSYM):
            fst[at, q] = jnp.where(sub2 == edge, rim[q : q + 1, :], roll(fst[source, q], turn, 0))
        for i in range(NV):
            xst[at, i] = jnp.where(
                sub2 == edge, rim[NSYM + i : NSYM + i + 1, :], roll(xst[source, i], turn, 0)
            )
        dst[at] = jnp.where(
            sub2 == edge, rim[NSYM + NV : NSYM + NV + 1, :], roll(dst[source], turn, 0)
        )

    def faces(t, carry):
        g = 0.25 * (fst[t] + fst[t + 1])
        f = 0.5 * (dst[t] + dst[t + 1])
        fs[t] = f
        for i in range(NV):
            for k in range(NV):
                e = g[SYM[i][k]]
                us[t, i, k] = e - f if i == k else e
                ls[t, i, k] = -e - f if i == k else -e
        return carry

    lax.fori_loop(0, GROUP + 1, faces, 0)

    zero = jnp.zeros((GROUP, 128), f32)
    for i in range(NV):
        for k in range(2 * NV):
            wc[0, i, k] = zero - 1.0 if i == k else zero
    for t in range(GROUP):
        dst[t] = fs[t] + time_ref[pl.ds(t, GROUP, stride=GROUP), :] + fs[t + 1]

    def forward(t, carry):
        diag = dst[t]
        low = [[ls[t, i, k] for k in range(NV)] for i in range(NV)]
        prod = mm(low, [wc[t, i] for i in range(NV)])
        m = [
            [(diag - prod[i][NV + k]) if i == k else -prod[i][NV + k] for k in range(NV)]
            for i in range(NV)
        ]
        inv = inverse(m)
        for i in range(NV):
            for k in range(NV):
                pinv[t, k, i] = inv[i][k]
        w = mm(inv, [-prod[i][0:NV] for i in range(NV)])
        c = mm(inv, [us[t + 1, i] for i in range(NV)])
        for i in range(NV):
            wc[t + 1, i, 0:NV] = w[i]
            wc[t + 1, i, NV:] = c[i]
        return carry

    lax.fori_loop(0, GROUP, forward, 0)

    for i in range(NV):
        hg[GROUP - 1, i] = wc[GROUP, i]

    def spikes(step, carry):
        t = GROUP - 2 - step
        c = [[wc[t + 1, i, NV + k] for k in range(NV)] for i in range(NV)]
        prod = mm(c, [hg[t + 1, i] for i in range(NV)])
        for i in range(NV):
            hg[t, i, 0:NV] = wc[t + 1, i, 0:NV] - prod[i][0:NV]
            hg[t, i, NV:] = -prod[i][NV:]
        return carry

    lax.fori_loop(0, GROUP - 1, spikes, 0)

    for c in copies_span:
        c.wait()
    no_prev = span == 0
    no_next = span == n_span - 1
    d = jnp.zeros((NV, GROUP, 128), f32)
    for t in range(GROUP):
        rows = pl.ds(t, GROUP, stride=GROUP)
        before = jnp.where(no_prev, 0.0, span_in[0, :, rows, :])
        after = jnp.where(no_next, 0.0, span_in[1, :, rows, :])
        rhs = -0.5 * (xst[t + 2] - xst[t])
        rhs = rhs + span_weight * (after - 2.0 * state_ref[:, rows, :] + before)
        for k in range(NV):
            rhs = rhs - ls[t, k] * d[k][None]
        d = pinv[t, 0] * rhs[0][None]
        for k in range(1, NV):
            d = d + pinv[t, k] * rhs[k][None]
        es[t] = d
    e = d
    for t in range(GROUP - 2, -1, -1):
        rows = [
            es[t, i] - jnp.sum(wc[t + 1, i, NV:] * e, axis=0) for i in range(NV)
        ]
        for i in range(NV):
            es[t, i] = rows[i]
        e = es[t]

    for which, t in ((0, 0), (1, GROUP - 1)):
        for i in range(NV):
            seg1[which, i, 0 : 2 * NV] = hg[t, i]
            seg1[which, i, 2 * NV] = es[t, i]
    tree_up(seg1, la1, fb1, 1, GROUP, 1)

    def two_port_rows(seg):
        for which in range(2):
            for i in range(NV):
                for c in range(2 * NV + 1):
                    r = (which * NV + i) * (2 * NV + 1) + c
                    tmp[r // 8, r % 8 : r % 8 + 1, :] = seg[which, i, c, 0:1, :]

    def two_port_load(seg, landed):
        for s in range(GROUP):
            for r in range(PACKS):
                tmp[r, s : s + 1, :] = landed[s, r]
        packed = swap_blocks(tmp[...])
        for which in range(2):
            for i in range(NV):
                for c in range(2 * NV + 1):
                    r = (which * NV + i) * (2 * NV + 1) + c
                    seg[which, i, c] = packed[r // 8, r % 8 : r % 8 + 1, :]

    for r in (110, 111):
        tmp[r // 8, r % 8 : r % 8 + 1, :] = jnp.zeros((1, 128), f32)
    two_port_rows(seg1)
    packed = swap_blocks(tmp[...])
    for s in range(GROUP):
        for r in range(PACKS):
            a_out[s, r] = packed[r, s : s + 1, :]
    copies = []
    for o in range(1, GROUP):
        copies.append(
            pltpu.make_async_remote_copy(
                src_ref=a_out.at[lax.rem(member + o, GROUP)], dst_ref=a_in.at[member],
                send_sem=a_sem.at[0, o], recv_sem=a_sem.at[1, o],
                device_id=(members[o - 1], span), device_id_type=MESH,
            )
        )
        copies[-1].start()
    a_in[member] = a_out[member]
    for c in copies:
        c.wait()
    two_port_load(seg2, a_in)
    tree_up(seg2, la2, fb2, 2, 128, WIDE)

    two_port_rows(seg2)
    packed = swap_blocks(tmp[...])
    for r in range(PACKS):
        b_out[r] = packed[r, 0:1, :]
    copies = []
    for o in range(1, GROUP):
        copies.append(
            pltpu.make_async_remote_copy(
                src_ref=b_out, dst_ref=b_in.at[plane],
                send_sem=b_sem.at[0, o], recv_sem=b_sem.at[1, o],
                device_id=(planes[o - 1], span), device_id_type=MESH,
            )
        )
        copies[-1].start()
    b_in[plane] = b_out[...]
    for c in copies:
        c.wait()
    two_port_load(seg3, b_in)
    tree_up(seg3, la3, fb3, 2, 128, WIDE)

    lane = lax.broadcasted_iota(jnp.int32, (NV, 1, 128), 2)
    nothing = jnp.zeros((NV, 1, 128), f32)
    p, n = tree_down(nothing, nothing, la3, fb3, 2, WIDE, lane)
    own = lax.rem(128 - plane * WIDE, 128)
    p = roll(p, own, 2)
    n = roll(n, own, 2)
    p, n = tree_down(p, n, la2, fb2, 2, WIDE, lane)

    for i in range(NV):
        tmp[0, i : i + 1, :] = p[i]
        tmp[1, i : i + 1, :] = n[i]
    packed = swap_blocks(tmp[0:2])
    for s in range(GROUP):
        for r in range(2):
            c_out[s, r] = packed[r, s : s + 1, :]
    copies = []
    for o in range(1, GROUP):
        copies.append(
            pltpu.make_async_remote_copy(
                src_ref=c_out.at[lax.rem(member + o, GROUP)], dst_ref=c_in.at[member],
                send_sem=c_sem.at[0, o], recv_sem=c_sem.at[1, o],
                device_id=(members[o - 1], span), device_id_type=MESH,
            )
        )
        copies[-1].start()
    c_in[member] = c_out[member]
    for c in copies:
        c.wait()
    for s in range(GROUP):
        for r in range(2):
            tmp[r, s : s + 1, :] = c_in[s, r]
    packed = swap_blocks(tmp[0:2])
    p = jnp.concatenate(
        [jnp.broadcast_to(packed[0, i : i + 1, :], (GROUP, 128))[None] for i in range(NV)], axis=0
    )
    n = jnp.concatenate(
        [jnp.broadcast_to(packed[1, i : i + 1, :], (GROUP, 128))[None] for i in range(NV)], axis=0
    )
    pos = lax.broadcasted_iota(jnp.int32, (NV, GROUP, 128), 1)
    p, n = tree_down(p, n, la1, fb1, 1, 1, pos)
    pn = jnp.concatenate([p, n], axis=0)
    for t in range(GROUP):
        for i in range(NV):
            out_ref[i, pl.ds(t, GROUP, stride=GROUP), :] = es[t, i] - jnp.sum(
                hg[t, i] * pn, axis=0
            )


def per_device(jacobian, state, metric, dissipation, time_term):
    nv = state.shape[0]
    points, lines = metric.shape[1:]
    vmem = pl.BlockSpec(memory_space=pltpu.VMEM)
    tile = (GROUP, lines)

    def two_port(tile):
        return [
            pltpu.VMEM((2, nv, 2 * nv + 1) + tile, f32),
            pltpu.VMEM((3, nv, 2 * nv + 1) + tile, f32),
            pltpu.VMEM((3, nv, 2 * nv + 1) + tile, f32),
        ]

    update = pl.pallas_call(
        kernel,
        out_shape=jax.ShapeDtypeStruct((nv, points, lines), f32),
        in_specs=[vmem] * 5,
        out_specs=vmem,
        scratch_shapes=[
            pltpu.VMEM((NSYM, points, lines), f32),
            pltpu.VMEM((nv, points, lines), f32),
            pltpu.VMEM((GROUP + 2, NSYM) + tile, f32),
            pltpu.VMEM((GROUP + 2,) + tile, f32),
            pltpu.VMEM((GROUP + 2, nv) + tile, f32),
            pltpu.VMEM((GROUP + 1, nv, nv) + tile, f32),
            pltpu.VMEM((GROUP + 1, nv, nv) + tile, f32),
            pltpu.VMEM((GROUP + 1,) + tile, f32),
            pltpu.VMEM((2, 24, lines), f32),
            pltpu.VMEM((2, 24, lines), f32),
            pltpu.VMEM((2, nv, points, lines), f32),
            pltpu.VMEM((GROUP + 1, nv, 2 * nv) + tile, f32),
            pltpu.VMEM((GROUP, nv, nv) + tile, f32),
            pltpu.VMEM((GROUP, nv, 2 * nv) + tile, f32),
            pltpu.VMEM((GROUP, nv) + tile, f32),
            *two_port(tile),
            *two_port((1, lines)),
            *two_port((1, lines)),
            pltpu.VMEM((PACKS,) + tile, f32),
            pltpu.VMEM((GROUP, PACKS, 1, lines), f32),
            pltpu.VMEM((GROUP, PACKS, 1, lines), f32),
            pltpu.VMEM((PACKS, 1, lines), f32),
            pltpu.VMEM((GROUP, PACKS, 1, lines), f32),
            pltpu.VMEM((GROUP, 2, 1, lines), f32),
            pltpu.VMEM((GROUP, 2, 1, lines), f32),
            pltpu.SemaphoreType.DMA((2, 2)),
            pltpu.SemaphoreType.DMA((2, 2)),
            pltpu.SemaphoreType.DMA((2, GROUP)),
            pltpu.SemaphoreType.DMA((2, GROUP)),
            pltpu.SemaphoreType.DMA((2, GROUP)),
        ],
        compiler_params=pltpu.CompilerParams(collective_id=0, has_side_effects=True),
        name="sweep",
    )(
        jacobian.reshape((nv, nv, points, lines)),
        state.reshape((nv, points, lines)),
        metric.reshape((points, lines)),
        dissipation.reshape((points, lines)),
        time_term.reshape((points, lines)),
    )
    return update.reshape(state.shape)


def solution(mesh):
    return jax.shard_map(
        per_device,
        mesh=mesh,
        in_specs=(
            P(None, None, "span", "line", None),
            P(None, "span", "line", None),
            P("span", "line", None),
            P("span", "line", None),
            P("span", "line", None),
        ),
        out_specs=P(None, "span", "line", None),
        check_vma=False,
    )
```

profile of v0, /device:TPU:1, one launch (start us, length us, event | category | flops | bytes accessed | tf_op | source)
XLA Modules:
  0.0 41.8 jit_solution(12586967178995896721)
XLA Ops:
  0.0 40.2 %sweep.1 = f32[5,64,128]{2,1,0:T(8,128)} custom-call(bf16[5,5,64,128]{3,2,1,0:T(8,128)(2,1)} %bitcast.9, f32[5,64,128]{2,1,0:T(8,128)} %bitcast.10, f32[64,128]{1,0:T(8,128)} %bitcast.11, f32[64,128]{1,0:T(8,128)} %bitcast.12, f32[64,128]{1,0:T(8,128)} %bitcast.13), custom_call_target="tpu_custom_call" | custom-call | tf_op jit(solution)/shard_map/sweep/pallas_call | solution.py:433
  40.2 1.6 %copy.8 = f32[5,1,64,128]{3,2,1,0:T(8,128)} copy(f32[5,1,64,128]{3,2,1,0:T(8,128)} %bitcast.8) | data formatting | bytes 327680
where the time goes:
time: 41.9 us; the launch traced here: 41.8 us
  Pallas kernels  40.2 us (96%)
  local copies, waits for them, and re-layouts  1.59 us (4%)
    pallas_call x1, Pallas kernels, per_device(): pl.pallas_call(kernel, out_shape=jax.ShapeDtypeStruct((nv, points, lines)...  40.2 us
    unnamed x1, local copies, waits for them, and re-layouts  1.59 us

commit v1 on v0

--- a/solution.py
+++ b/solution.py
@@ -11,7 +11,7 @@
 NV = 5
 GROUP = 8
 WIDE = 16
-PACKS = 14
+PACKS = 15
 PAIRS = [(i, j) for i in range(NV) for j in range(i, NV)]
 SYM = [[PAIRS.index((min(i, j), max(i, j))) for j in range(NV)] for i in range(NV)]
 NSYM = len(PAIRS)
@@ -49,35 +49,40 @@
     return m
 
 
-def tree_up(seg, la_ref, fb_ref, axis, size, base):
+def matvec(columns, v):
+    acc = columns[0] * v[0][None]
+    for k in range(1, NV):
+        acc = acc + columns[k] * v[k][None]
+    return acc
+
+
+def tree_up_matrices(seg, la_ref, fb_ref, keep):
     def body(level, carry):
-        back = size - lax.shift_left(jnp.int32(base), level)
+        back = GROUP - lax.shift_left(jnp.int32(1), level)
         fa = [seg[0, i] for i in range(NV)]
         la = [seg[1, i] for i in range(NV)]
-        fb = [roll(x, back, axis) for x in fa]
-        lb = [roll(x, back, axis) for x in la]
+        fb = [roll(x, back, 1) for x in fa]
+        lb = [roll(x, back, 1) for x in la]
         t = mm([[la[i][NV + k] for k in range(NV)] for i in range(NV)], fb)
         eye = [[(1.0 if i == k else 0.0) - t[i][k] for k in range(NV)] for i in range(NV)]
         x = inverse(eye)
-        q = [
-            jnp.concatenate(
-                [la[i][0:NV], -t[i][NV : 2 * NV], la[i][2 * NV :] - t[i][2 * NV :]], axis=0
-            )
-            for i in range(NV)
-        ]
+        q = [jnp.concatenate([la[i][0:NV], -t[i][NV:]], axis=0) for i in range(NV)]
         ela = mm(x, q)
         r = mm([[fb[i][k] for k in range(NV)] for i in range(NV)], ela)
-        efb = [
-            jnp.concatenate([-r[i][0:NV], fb[i][NV:] - r[i][NV:]], axis=0) for i in range(NV)
-        ]
+        efb = [jnp.concatenate([-r[i][0:NV], fb[i][NV:] - r[i][NV:]], axis=0) for i in range(NV)]
         s = mm([[fa[i][NV + k] for k in range(NV)] for i in range(NV)], efb)
         y = mm([[lb[i][k] for k in range(NV)] for i in range(NV)], ela)
         for i in range(NV):
-            la_ref[level, i] = ela[i]
-            fb_ref[level, i] = efb[i]
+            for k in range(NV):
+                keep[level, 0, k, i] = la[i][NV + k]
+                keep[level, 1, k, i] = x[i][k]
+                keep[level, 2, k, i] = fb[i][k]
+                keep[level, 3, k, i] = fa[i][NV + k]
+                keep[level, 4, k, i] = lb[i][k]
+            la_ref[level, i, 0 : 2 * NV] = ela[i]
+            fb_ref[level, i, 0 : 2 * NV] = efb[i]
             seg[0, i, 0:NV] = fa[i][0:NV] - s[i][0:NV]
-            seg[0, i, NV : 2 * NV] = -s[i][NV : 2 * NV]
-            seg[0, i, 2 * NV :] = fa[i][2 * NV :] - s[i][2 * NV :]
+            seg[0, i, NV:] = -s[i][NV:]
             seg[1, i, 0:NV] = -y[i][0:NV]
             seg[1, i, NV:] = lb[i][NV:] - y[i][NV:]
         return carry
@@ -85,28 +90,101 @@
     lax.fori_loop(0, 3, body, 0)
 
 
-def tree_down(p, n, la_ref, fb_ref, axis, base, pos):
+def tree_up_rhs(f, l, la_ref, fb_ref, keep):
+    for level in range(3):
+        back = GROUP - (1 << level)
+        m = [[keep[level, w, k] for k in range(NV)] for w in range(5)]
+        fb = roll(f, back, 1)
+        lb = roll(l, back, 1)
+        la_c = matvec(m[1], l - matvec(m[0], fb))
+        fb_c = fb - matvec(m[2], la_c)
+        f = f - matvec(m[3], fb_c)
+        l = lb - matvec(m[4], la_c)
+        for i in range(NV):
+            la_ref[level, i, 2 * NV] = la_c[i]
+            fb_ref[level, i, 2 * NV] = fb_c[i]
+    return f, l
+
+
+def spread(ref, index, column):
+    return jnp.broadcast_to(
+        ref[index + (column // 8, slice(column % 8, column % 8 + 1), slice(None))], (GROUP, 128)
+    )
+
+
+def tree_up_lanes(seg, near, temp, la_ref, fb_ref):
+    tile = lax.broadcasted_iota(jnp.int32, (2, GROUP, 128), 0)
+    column = tile * GROUP + lax.broadcasted_iota(jnp.int32, (2, GROUP, 128), 1)
+    not_n = (column < NV) | (column == 2 * NV)
+    not_p = column >= NV
+
+    def body(level, carry):
+        back = 128 - lax.shift_left(jnp.int32(WIDE), level)
+        fa = [seg[0, i] for i in range(NV)]
+        la = [seg[1, i] for i in range(NV)]
+        fb = [roll(x, back, 2) for x in fa]
+        lb = [roll(x, back, 2) for x in la]
+        for i in range(NV):
+            near[0, i] = fb[i]
+            near[1, i] = lb[i]
+        left = lambda ref, which, first: [
+            [spread(ref, (which, i), first + k) for k in range(NV)] for i in range(NV)
+        ]
+        t = mm(left(seg, 1, NV), fb)
+        for i in range(NV):
+            temp[i] = t[i]
+        eye = [
+            [(1.0 if i == k else 0.0) - spread(temp, (i,), k) for k in range(NV)]
+            for i in range(NV)
+        ]
+        x = inverse(eye)
+        ela = mm(
+            x, [jnp.where(not_n, la[i], 0.0) - jnp.where(not_p, t[i], 0.0) for i in range(NV)]
+        )
+        r = mm(left(near, 0, 0), ela)
+        efb = [jnp.where(not_p, fb[i], 0.0) - r[i] for i in range(NV)]
+        s = mm(left(seg, 0, NV), efb)
+        y = mm(left(near, 1, 0), ela)
+        for i in range(NV):
+            la_ref[level, i] = ela[i]
+            fb_ref[level, i] = efb[i]
+            seg[0, i] = jnp.where(not_n, fa[i], 0.0) - s[i]
+            seg[1, i] = jnp.where(not_p, lb[i], 0.0) - y[i]
+        return carry
+
+    lax.fori_loop(0, 3, body, 0)
+
+
+def tree_down(p, n, la, fb, axis, base, pos):
     for level in (2, 1, 0):
         shift = base << level
-        pn = jnp.concatenate([p, n], axis=0)
-        la = []
-        fb = []
-        for i in range(NV):
-            la.append(
-                la_ref[level, i, 2 * NV :]
-                - jnp.sum(la_ref[level, i, 0 : 2 * NV] * pn, axis=0, keepdims=True)
-            )
-            fb.append(
-                fb_ref[level, i, 2 * NV :]
-                - jnp.sum(fb_ref[level, i, 0 : 2 * NV] * pn, axis=0, keepdims=True)
-            )
-        la = jnp.concatenate(la, axis=0)
-        fb = jnp.concatenate(fb, axis=0)
         second = (pos & shift) != 0
-        p, n = (
-            jnp.where(second, roll(la, shift, axis), p),
-            jnp.where(second, roll(n, shift, axis), fb),
-        )
+        value = []
+        for get in (la, fb):
+            rows = []
+            for i in range(NV):
+                row = get(level, i, 2 * NV)
+                if p is not None:
+                    terms = [get(level, i, k) * p[k] for k in range(NV)]
+                    terms += [get(level, i, NV + k) * n[k] for k in range(NV)]
+                    while len(terms) > 1:
+                        terms = [
+                            terms[j] + terms[j + 1] if j + 1 < len(terms) else terms[j]
+                            for j in range(0, len(terms), 2)
+                        ]
+                    row = row - terms[0]
+                rows.append(row)
+            value.append(rows)
+        new_p = []
+        new_n = []
+        for i in range(NV):
+            new_p.append(
+                jnp.where(second, roll(value[0][i], shift, axis), 0.0 if p is None else p[i])
+            )
+            new_n.append(
+                jnp.where(second, 0.0 if n is None else roll(n[i], shift, axis), value[1][i])
+            )
+        p, n = new_p, new_n
     return p, n
 
 
@@ -125,13 +203,14 @@
 
 
 def kernel(
-    jac_ref, state_ref, metric_ref, diss_ref, time_ref, out_ref,
+    jac_hbm, state_hbm, metric_hbm, diss_hbm, time_hbm, out_ref,
+    jac_ref, state_ref, metric_ref, diss_ref, time_ref,
     sym_ref, flux_ref, fst, dst, xst, ls, us, fs,
     rim_out, rim_in, span_in,
     wc, pinv, hg, es,
-    seg1, la1, fb1, seg2, la2, fb2, seg3, la3, fb3,
+    seg1, la1, fb1, keep, seg2, la2, fb2, seg3, la3, fb3, near, temp,
     tmp, a_out, a_in, b_out, b_in, c_out, c_in,
-    span_sem, rim_sem, a_sem, b_sem, c_sem,
+    load_sem, span_sem, rim_sem, a_sem, b_sem, c_sem,
 ):
     line = lax.axis_index("line")
     span = lax.axis_index("span")
@@ -146,12 +225,29 @@
     members = [plane * GROUP + lax.rem(member + o, GROUP) for o in range(1, GROUP)]
     planes = [lax.rem(plane + o, GROUP) * GROUP + member for o in range(1, GROUP)]
 
+    loads = [
+        pltpu.make_async_copy(source, target, load_sem.at[i])
+        for i, (source, target) in enumerate(
+            (
+                (jac_hbm, jac_ref),
+                (state_hbm, state_ref),
+                (metric_hbm, metric_ref),
+                (diss_hbm, diss_ref),
+                (time_hbm, time_ref),
+            )
+        )
+    ]
+    for c in loads:
+        c.start()
+
     peers = [(line, span_next), (line, span_prev), (line_next, span), (line_prev, span)]
     peers += [(x, span) for x in members] + [(x, span) for x in planes]
     barrier = pltpu.get_barrier_semaphore()
     for peer in peers:
         pl.semaphore_signal(barrier, inc=1, device_id=peer, device_id_type=MESH)
 
+    for c in loads:
+        c.wait()
     metric = metric_ref[...]
     for q, (i, j) in enumerate(PAIRS):
         if i == j:
@@ -189,7 +285,7 @@
     for side, target in ((0, span_next), (1, span_prev)):
         copies_span.append(
             pltpu.make_async_remote_copy(
-                src_ref=state_ref, dst_ref=span_in.at[side],
+                src_ref=state_hbm, dst_ref=span_in.at[side],
                 send_sem=span_sem.at[0, side], recv_sem=span_sem.at[1, side],
                 device_id=(line, target), device_id_type=MESH,
             )
@@ -200,7 +296,19 @@
         fst[t + 1] = sym_ref[:, pl.ds(t, GROUP, stride=GROUP), :]
         xst[t + 1] = flux_ref[:, pl.ds(t, GROUP, stride=GROUP), :]
         dst[t + 1] = diss_ref[pl.ds(t, GROUP, stride=GROUP), :]
-    sub3 = lax.broadcasted_iota(jnp.int32, (1, GROUP, 128), 1)
+    def faces(t, carry):
+        g = 0.25 * (fst[t] + fst[t + 1])
+        f = 0.5 * (dst[t] + dst[t + 1])
+        fs[t] = f
+        for i in range(NV):
+            for k in range(NV):
+                e = g[SYM[i][k]]
+                us[t, i, k] = e - f if i == k else e
+                ls[t, i, k] = -e - f if i == k else -e
+        return carry
+
+    lax.fori_loop(1, GROUP, faces, 0)
+
     sub2 = lax.broadcasted_iota(jnp.int32, (GROUP, 128), 0)
     for c in copies_rim:
         c.wait()
@@ -221,18 +329,7 @@
             sub2 == edge, rim[NSYM + NV : NSYM + NV + 1, :], roll(dst[source], turn, 0)
         )
 
-    def faces(t, carry):
-        g = 0.25 * (fst[t] + fst[t + 1])
-        f = 0.5 * (dst[t] + dst[t + 1])
-        fs[t] = f
-        for i in range(NV):
-            for k in range(NV):
-                e = g[SYM[i][k]]
-                us[t, i, k] = e - f if i == k else e
-                ls[t, i, k] = -e - f if i == k else -e
-        return carry
-
-    lax.fori_loop(0, GROUP + 1, faces, 0)
+    lax.fori_loop(0, 2, lambda t, carry: faces(t * GROUP, carry), 0)
 
     zero = jnp.zeros((GROUP, 128), f32)
     for i in range(NV):
@@ -275,6 +372,24 @@
         return carry
 
     lax.fori_loop(0, GROUP - 1, spikes, 0)
+
+    for which, t in ((0, 0), (1, GROUP - 1)):
+        for i in range(NV):
+            seg1[which, i] = hg[t, i]
+    tree_up_matrices(seg1, la1, fb1, keep)
+
+    def slot(which, i, column):
+        if column < 8:
+            return which * NV + i, column
+        return 2 * NV + i, which * 3 + column - 8
+
+    for i in range(NV):
+        tmp[2 * NV + i, 6:8, :] = jnp.zeros((2, 128), f32)
+    for which in range(2):
+        for i in range(NV):
+            for c in range(2 * NV):
+                r, j = slot(which, i, c)
+                tmp[r, j : j + 1, :] = seg1[which, i, c, 0:1, :]
 
     for c in copies_span:
         c.wait()
@@ -302,33 +417,23 @@
             es[t, i] = rows[i]
         e = es[t]
 
-    for which, t in ((0, 0), (1, GROUP - 1)):
-        for i in range(NV):
-            seg1[which, i, 0 : 2 * NV] = hg[t, i]
-            seg1[which, i, 2 * NV] = es[t, i]
-    tree_up(seg1, la1, fb1, 1, GROUP, 1)
-
-    def two_port_rows(seg):
-        for which in range(2):
-            for i in range(NV):
-                for c in range(2 * NV + 1):
-                    r = (which * NV + i) * (2 * NV + 1) + c
-                    tmp[r // 8, r % 8 : r % 8 + 1, :] = seg[which, i, c, 0:1, :]
+    first, last = tree_up_rhs(es[0], es[GROUP - 1], la1, fb1, keep)
 
     def two_port_load(seg, landed):
         for s in range(GROUP):
             for r in range(PACKS):
                 tmp[r, s : s + 1, :] = landed[s, r]
         packed = swap_blocks(tmp[...])
-        for which in range(2):
-            for i in range(NV):
-                for c in range(2 * NV + 1):
-                    r = (which * NV + i) * (2 * NV + 1) + c
-                    seg[which, i, c] = packed[r // 8, r % 8 : r % 8 + 1, :]
-
-    for r in (110, 111):
-        tmp[r // 8, r % 8 : r % 8 + 1, :] = jnp.zeros((1, 128), f32)
-    two_port_rows(seg1)
+        for i in range(NV):
+            seg[0, i, 0] = packed[i]
+            seg[1, i, 0] = packed[NV + i]
+            seg[0, i, 1] = packed[2 * NV + i]
+            seg[1, i, 1] = roll(packed[2 * NV + i], GROUP - 3, 0)
+
+    for which, value in ((0, first), (1, last)):
+        for i in range(NV):
+            r, j = slot(which, i, 2 * NV)
+            tmp[r, j : j + 1, :] = value[i, 0:1, :]
     packed = swap_blocks(tmp[...])
     for s in range(GROUP):
         for r in range(PACKS):
@@ -347,10 +452,18 @@
     for c in copies:
         c.wait()
     two_port_load(seg2, a_in)
-    tree_up(seg2, la2, fb2, 2, 128, WIDE)
-
-    two_port_rows(seg2)
-    packed = swap_blocks(tmp[...])
+    tree_up_lanes(seg2, near, temp, la2, fb2)
+
+    packed = swap_blocks(
+        jnp.concatenate(
+            [seg2[0, :, 0], seg2[1, :, 0]]
+            + [
+                jnp.where(sub2 < 3, seg2[0, i, 1], roll(seg2[1, i, 1], 3, 0))[None]
+                for i in range(NV)
+            ],
+            axis=0,
+        )
+    )
     for r in range(PACKS):
         b_out[r] = packed[r, 0:1, :]
     copies = []
@@ -367,19 +480,21 @@
     for c in copies:
         c.wait()
     two_port_load(seg3, b_in)
-    tree_up(seg3, la3, fb3, 2, 128, WIDE)
-
-    lane = lax.broadcasted_iota(jnp.int32, (NV, 1, 128), 2)
-    nothing = jnp.zeros((NV, 1, 128), f32)
-    p, n = tree_down(nothing, nothing, la3, fb3, 2, WIDE, lane)
+    tree_up_lanes(seg3, near, temp, la3, fb3)
+
+    lane = lax.broadcasted_iota(jnp.int32, (GROUP, 128), 1)
+    get = lambda ref: lambda level, i, column: spread(ref, (level, i), column)
+    p, n = tree_down(None, None, get(la3), get(fb3), 1, WIDE, lane)
     own = lax.rem(128 - plane * WIDE, 128)
-    p = roll(p, own, 2)
-    n = roll(n, own, 2)
-    p, n = tree_down(p, n, la2, fb2, 2, WIDE, lane)
-
-    for i in range(NV):
-        tmp[0, i : i + 1, :] = p[i]
-        tmp[1, i : i + 1, :] = n[i]
+    p = [roll(x, own, 1) for x in p]
+    n = [roll(x, own, 1) for x in n]
+    p, n = tree_down(p, n, get(la2), get(fb2), 1, WIDE, lane)
+
+    for r, values in ((0, p), (1, n)):
+        tile = values[0]
+        for i in range(1, NV):
+            tile = jnp.where(sub2 == i, values[i], tile)
+        tmp[r] = tile
     packed = swap_blocks(tmp[0:2])
     for s in range(GROUP):
         for r in range(2):
@@ -401,15 +516,11 @@
         for r in range(2):
             tmp[r, s : s + 1, :] = c_in[s, r]
     packed = swap_blocks(tmp[0:2])
-    p = jnp.concatenate(
-        [jnp.broadcast_to(packed[0, i : i + 1, :], (GROUP, 128))[None] for i in range(NV)], axis=0
-    )
-    n = jnp.concatenate(
-        [jnp.broadcast_to(packed[1, i : i + 1, :], (GROUP, 128))[None] for i in range(NV)], axis=0
-    )
-    pos = lax.broadcasted_iota(jnp.int32, (NV, GROUP, 128), 1)
-    p, n = tree_down(p, n, la1, fb1, 1, 1, pos)
-    pn = jnp.concatenate([p, n], axis=0)
+    p = [jnp.broadcast_to(packed[0, i : i + 1, :], (GROUP, 128)) for i in range(NV)]
+    n = [jnp.broadcast_to(packed[1, i : i + 1, :], (GROUP, 128)) for i in range(NV)]
+    get = lambda ref: lambda level, i, column: ref[level, i, column]
+    p, n = tree_down(p, n, get(la1), get(fb1), 0, 1, sub2)
+    pn = jnp.concatenate([x[None] for x in p + n], axis=0)
     for t in range(GROUP):
         for i in range(NV):
             out_ref[i, pl.ds(t, GROUP, stride=GROUP), :] = es[t, i] - jnp.sum(
@@ -423,19 +534,17 @@
     vmem = pl.BlockSpec(memory_space=pltpu.VMEM)
     tile = (GROUP, lines)
 
-    def two_port(tile):
-        return [
-            pltpu.VMEM((2, nv, 2 * nv + 1) + tile, f32),
-            pltpu.VMEM((3, nv, 2 * nv + 1) + tile, f32),
-            pltpu.VMEM((3, nv, 2 * nv + 1) + tile, f32),
-        ]
-
     update = pl.pallas_call(
         kernel,
         out_shape=jax.ShapeDtypeStruct((nv, points, lines), f32),
-        in_specs=[vmem] * 5,
+        in_specs=[pl.BlockSpec(memory_space=pl.ANY)] * 5,
         out_specs=vmem,
         scratch_shapes=[
+            pltpu.VMEM((nv, nv, points, lines), jacobian.dtype),
+            pltpu.VMEM((nv, points, lines), f32),
+            pltpu.VMEM((points, lines), f32),
+            pltpu.VMEM((points, lines), f32),
+            pltpu.VMEM((points, lines), f32),
             pltpu.VMEM((NSYM, points, lines), f32),
             pltpu.VMEM((nv, points, lines), f32),
             pltpu.VMEM((GROUP + 2, NSYM) + tile, f32),
@@ -451,9 +560,18 @@
             pltpu.VMEM((GROUP, nv, nv) + tile, f32),
             pltpu.VMEM((GROUP, nv, 2 * nv) + tile, f32),
             pltpu.VMEM((GROUP, nv) + tile, f32),
-            *two_port(tile),
-            *two_port((1, lines)),
-            *two_port((1, lines)),
+            pltpu.VMEM((2, nv, 2 * nv) + tile, f32),
+            pltpu.VMEM((3, nv, 2 * nv + 1) + tile, f32),
+            pltpu.VMEM((3, nv, 2 * nv + 1) + tile, f32),
+            pltpu.VMEM((3, 5, nv, nv) + tile, f32),
+            pltpu.VMEM((2, nv, 2) + tile, f32),
+            pltpu.VMEM((3, nv, 2) + tile, f32),
+            pltpu.VMEM((3, nv, 2) + tile, f32),
+            pltpu.VMEM((2, nv, 2) + tile, f32),
+            pltpu.VMEM((3, nv, 2) + tile, f32),
+            pltpu.VMEM((3, nv, 2) + tile, f32),
+            pltpu.VMEM((2, nv, 2) + tile, f32),
+            pltpu.VMEM((nv, 2) + tile, f32),
             pltpu.VMEM((PACKS,) + tile, f32),
             pltpu.VMEM((GROUP, PACKS, 1, lines), f32),
             pltpu.VMEM((GROUP, PACKS, 1, lines), f32),
@@ -461,6 +579,7 @@
             pltpu.VMEM((GROUP, PACKS, 1, lines), f32),
             pltpu.VMEM((GROUP, 2, 1, lines), f32),
             pltpu.VMEM((GROUP, 2, 1, lines), f32),
+            pltpu.SemaphoreType.DMA((5,)),
             pltpu.SemaphoreType.DMA((2, 2)),
             pltpu.SemaphoreType.DMA((2, 2)),
             pltpu.SemaphoreType.DMA((2, GROUP)),

time: 41.9 us -> 38.5 us (0.919)
  Pallas kernels: 40.2 us -> 36.8 us
    pallas_call x1, Pallas kernels: 40.2 us -> 36.8 us  [per_device(): pl.pallas_call(kernel, out_shape=jax.ShapeDtypeStruct((nv, points, lines)...]
where the time goes in v1:
time: 38.5 us; the launch traced here: 38.4 us
  Pallas kernels  36.8 us (96%)
  local copies, waits for them, and re-layouts  1.59 us (4%)
    pallas_call x1, Pallas kernels, per_device(): pl.pallas_call(kernel, out_shape=jax.ShapeDtypeStruct((nv, points, lines)...  36.8 us
    unnamed x1, local copies, waits for them, and re-layouts  1.59 us

profile of v1, /device:TPU:1, one launch (start us, length us, event | category | flops | bytes accessed | tf_op | source)
XLA Modules:
  0.0 38.4 jit_solution(11059654434317885704)
XLA Ops:
  0.0 36.8 %sweep.1 = f32[5,64,128]{2,1,0:T(8,128)} custom-call(bf16[5,5,64,128]{3,2,1,0:T(8,128)(2,1)} %bitcast.9, f32[5,64,128]{2,1,0:T(8,128)} %bitcast.10, f32[64,128]{1,0:T(8,128)} %bitcast.11, f32[64,128]{1,0:T(8,128)} %bitcast.12, f32[64,128]{1,0:T(8,128)} %bitcast.13), custom_call_target="tpu_custom_call" | custom-call | tf_op jit(solution)/shard_map/sweep/pallas_call | solution.py:537
  36.8 1.6 %copy.8 = f32[5,1,64,128]{3,2,1,0:T(8,128)} copy(f32[5,1,64,128]{3,2,1,0:T(8,128)} %bitcast.8) | data formatting | bytes 327680

commit v2 on v1

--- a/solution.py
+++ b/solution.py
@@ -210,7 +210,7 @@
     wc, pinv, hg, es,
     seg1, la1, fb1, keep, seg2, la2, fb2, seg3, la3, fb3, near, temp,
     tmp, a_out, a_in, b_out, b_in, c_out, c_in,
-    load_sem, span_sem, rim_sem, a_sem, b_sem, c_sem,
+    line_sem, plane_sem, load_sem, span_sem, rim_sem, a_sem, b_sem, c_sem,
 ):
     line = lax.axis_index("line")
     span = lax.axis_index("span")
@@ -222,6 +222,7 @@
     line_prev = lax.rem(line + n_line - 1, n_line)
     span_next = lax.rem(span + 1, n_span)
     span_prev = lax.rem(span + n_span - 1, n_span)
+    far_first = sorted(range(1, GROUP), key=lambda o: abs(o - GROUP // 2))
     members = [plane * GROUP + lax.rem(member + o, GROUP) for o in range(1, GROUP)]
     planes = [lax.rem(plane + o, GROUP) * GROUP + member for o in range(1, GROUP)]
 
@@ -241,7 +242,7 @@
         c.start()
 
     peers = [(line, span_next), (line, span_prev), (line_next, span), (line_prev, span)]
-    peers += [(x, span) for x in members] + [(x, span) for x in planes]
+    peers += [(planes[0], span), (planes[-1], span)]
     barrier = pltpu.get_barrier_semaphore()
     for peer in peers:
         pl.semaphore_signal(barrier, inc=1, device_id=peer, device_id_type=MESH)
@@ -271,6 +272,23 @@
 
     pl.semaphore_wait(barrier, len(peers))
 
+    def greet(sem, size, step, position, spread_by, round_at):
+        reach = (1 << round_at)
+        for other in (lax.rem(position + reach, size), lax.rem(position + size - reach, size)):
+            pl.semaphore_signal(
+                sem.at[round_at], inc=1, device_id=(other * step + spread_by, span),
+                device_id_type=MESH,
+            )
+
+    def greet_line(round_at):
+        greet(line_sem, n_line, 1, line, 0, round_at)
+
+    def greet_plane(round_at):
+        greet(plane_sem, n_line // GROUP, GROUP, plane, member, round_at)
+
+    greet_line(0)
+    greet_plane(0)
+
     copies_rim = []
     for side, target in ((0, line_next), (1, line_prev)):
         copies_rim.append(
@@ -358,6 +376,10 @@
         return carry
 
     lax.fori_loop(0, GROUP, forward, 0)
+    pl.semaphore_wait(line_sem.at[0], 2)
+    pl.semaphore_wait(plane_sem.at[0], 2)
+    greet_line(1)
+    greet_plane(1)
 
     for i in range(NV):
         hg[GROUP - 1, i] = wc[GROUP, i]
@@ -372,6 +394,8 @@
         return carry
 
     lax.fori_loop(0, GROUP - 1, spikes, 0)
+    pl.semaphore_wait(line_sem.at[1], 2)
+    greet_line(2)
 
     for which, t in ((0, 0), (1, GROUP - 1)):
         for i in range(NV):
@@ -391,6 +415,8 @@
                 r, j = slot(which, i, c)
                 tmp[r, j : j + 1, :] = seg1[which, i, c, 0:1, :]
 
+    pl.semaphore_wait(line_sem.at[2], 2)
+    pl.semaphore_wait(plane_sem.at[1], 2)
     for c in copies_span:
         c.wait()
     no_prev = span == 0
@@ -439,7 +465,7 @@
         for r in range(PACKS):
             a_out[s, r] = packed[r, s : s + 1, :]
     copies = []
-    for o in range(1, GROUP):
+    for o in far_first:
         copies.append(
             pltpu.make_async_remote_copy(
                 src_ref=a_out.at[lax.rem(member + o, GROUP)], dst_ref=a_in.at[member],
@@ -467,7 +493,7 @@
     for r in range(PACKS):
         b_out[r] = packed[r, 0:1, :]
     copies = []
-    for o in range(1, GROUP):
+    for o in far_first:
         copies.append(
             pltpu.make_async_remote_copy(
                 src_ref=b_out, dst_ref=b_in.at[plane],
@@ -500,7 +526,7 @@
         for r in range(2):
             c_out[s, r] = packed[r, s : s + 1, :]
     copies = []
-    for o in range(1, GROUP):
+    for o in far_first:
         copies.append(
             pltpu.make_async_remote_copy(
                 src_ref=c_out.at[lax.rem(member + o, GROUP)], dst_ref=c_in.at[member],
@@ -536,7 +562,7 @@
 
     update = pl.pallas_call(
         kernel,
-        out_shape=jax.ShapeDtypeStruct((nv, points, lines), f32),
+        out_shape=pltpu.VMEM((nv, points, lines), f32),
         in_specs=[pl.BlockSpec(memory_space=pl.ANY)] * 5,
         out_specs=vmem,
         scratch_shapes=[
@@ -579,6 +605,8 @@
             pltpu.VMEM((GROUP, PACKS, 1, lines), f32),
             pltpu.VMEM((GROUP, 2, 1, lines), f32),
             pltpu.VMEM((GROUP, 2, 1, lines), f32),
+            pltpu.SemaphoreType.REGULAR((3,)),
+            pltpu.SemaphoreType.REGULAR((2,)),
             pltpu.SemaphoreType.DMA((5,)),
             pltpu.SemaphoreType.DMA((2, 2)),
             pltpu.SemaphoreType.DMA((2, 2)),

time: 38.5 us -> 37.8 us (0.982)
  local copies, waits for them, and re-layouts: 1.59 us -> 0.67 us
    unnamed x1, local copies, waits for them, and re-layouts: 1.59 us -> 0.67 us
where the time goes in v2:
time: 37.8 us; the launch traced here: 37.7 us
  Pallas kernels  37 us (98%)
  local copies, waits for them, and re-layouts  0.67 us (2%)
    pallas_call x1, Pallas kernels, per_device(): pl.pallas_call(kernel, out_shape=pltpu.VMEM((nv, points, lines), f32), in...  37 us

profile of v2, /device:TPU:1, one launch (start us, length us, event | category | flops | bytes accessed | tf_op | source)
XLA Modules:
  0.0 37.7 jit_solution(6982244095173095780)
XLA Ops:
  0.0 37.0 %sweep.1 = f32[5,64,128]{2,1,0:T(8,128)S(1)} custom-call(bf16[5,5,64,128]{3,2,1,0:T(8,128)(2,1)} %bitcast.9, f32[5,64,128]{2,1,0:T(8,128)} %bitcast.10, f32[64,128]{1,0:T(8,128)} %bitcast.11, f32[64,128]{1,0:T(8,128)} %bitcast.12, f32[64,128]{1,0:T(8,128)} %bitcast.13), custom_call_target="tpu_custom_call" | custom-call | tf_op jit(solution)/shard_map/sweep/pallas_call | solution.py:563
  37.0 0.7 %copy.8 = f32[5,1,64,128]{3,2,1,0:T(8,128)} copy(f32[5,1,64,128]{3,2,1,0:T(8,128)S(1)} %bitcast.8) | data formatting | bytes 327680

commit v3 on v2

--- a/solution.py
+++ b/solution.py
@@ -208,7 +208,7 @@
     sym_ref, flux_ref, fst, dst, xst, ls, us, fs,
     rim_out, rim_in, span_in,
     wc, pinv, hg, es,
-    seg1, la1, fb1, keep, seg2, la2, fb2, seg3, la3, fb3, near, temp,
+    seg1, la1, fb1, keep, dev, part, ends, mean, small, seg2, la2, fb2, seg3, la3, fb3, near, temp,
     tmp, a_out, a_in, b_out, b_in, c_out, c_in,
     line_sem, plane_sem, load_sem, span_sem, rim_sem, a_sem, b_sem, c_sem,
 ):
@@ -314,6 +314,13 @@
         fst[t + 1] = sym_ref[:, pl.ds(t, GROUP, stride=GROUP), :]
         xst[t + 1] = flux_ref[:, pl.ds(t, GROUP, stride=GROUP), :]
         dst[t + 1] = diss_ref[pl.ds(t, GROUP, stride=GROUP), :]
+    sub2 = lax.broadcasted_iota(jnp.int32, (GROUP, 128), 0)
+    sub3 = lax.broadcasted_iota(jnp.int32, (1, GROUP, 128), 1)
+    fst[0] = roll(fst[GROUP], 1, 1)
+    fst[GROUP + 1] = roll(fst[1], GROUP - 1, 1)
+    dst[0] = roll(dst[GROUP], 1, 0)
+    dst[GROUP + 1] = roll(dst[1], GROUP - 1, 0)
+
     def faces(t, carry):
         g = 0.25 * (fst[t] + fst[t + 1])
         f = 0.5 * (dst[t] + dst[t + 1])
@@ -325,36 +332,20 @@
                 ls[t, i, k] = -e - f if i == k else -e
         return carry
 
-    lax.fori_loop(1, GROUP, faces, 0)
-
-    sub2 = lax.broadcasted_iota(jnp.int32, (GROUP, 128), 0)
-    for c in copies_rim:
-        c.wait()
-    first_device = line == 0
-    last_device = line == n_line - 1
-    for side, at, source, turn, edge, outside in (
-        (0, 0, GROUP, 1, 0, first_device),
-        (1, GROUP + 1, 1, GROUP - 1, GROUP - 1, last_device),
-    ):
-        rim = jnp.where(outside, 0.0, rim_in[side])
-        for q in range(NSYM):
-            fst[at, q] = jnp.where(sub2 == edge, rim[q : q + 1, :], roll(fst[source, q], turn, 0))
-        for i in range(NV):
-            xst[at, i] = jnp.where(
-                sub2 == edge, rim[NSYM + i : NSYM + i + 1, :], roll(xst[source, i], turn, 0)
-            )
-        dst[at] = jnp.where(
-            sub2 == edge, rim[NSYM + NV : NSYM + NV + 1, :], roll(dst[source], turn, 0)
-        )
-
-    lax.fori_loop(0, 2, lambda t, carry: faces(t * GROUP, carry), 0)
-
-    zero = jnp.zeros((GROUP, 128), f32)
-    for i in range(NV):
-        for k in range(2 * NV):
-            wc[0, i, k] = zero - 1.0 if i == k else zero
+    lax.fori_loop(0, GROUP + 1, faces, 0)
+
     for t in range(GROUP):
         dst[t] = fs[t] + time_ref[pl.ds(t, GROUP, stride=GROUP), :] + fs[t + 1]
+
+    first_row = sub2 == 0
+    last_row = sub2 == GROUP - 1
+    scale = 1.0 / dst[0]
+    for i in range(NV):
+        for k in range(NV):
+            same = 1.0 if i == k else 0.0
+            wc[1, i, k] = jnp.where(first_row, -same, ls[0, i, k] * scale)
+            wc[1, i, NV + k] = jnp.where(first_row, 0.0, us[1, i, k] * scale)
+            pinv[0, k, i] = jnp.where(first_row, 0.0, same * scale)
 
     def forward(t, carry):
         diag = dst[t]
@@ -375,7 +366,13 @@
             wc[t + 1, i, NV:] = c[i]
         return carry
 
-    lax.fori_loop(0, GROUP, forward, 0)
+    lax.fori_loop(1, GROUP, forward, 0)
+    for i in range(NV):
+        for k in range(NV):
+            same = 1.0 if i == k else 0.0
+            wc[GROUP, i, k] = jnp.where(last_row, 0.0, wc[GROUP, i, k])
+            wc[GROUP, i, NV + k] = jnp.where(last_row, -same, wc[GROUP, i, NV + k])
+            pinv[GROUP - 1, k, i] = jnp.where(last_row, 0.0, pinv[GROUP - 1, k, i])
     pl.semaphore_wait(line_sem.at[0], 2)
     pl.semaphore_wait(plane_sem.at[0], 2)
     greet_line(1)
@@ -397,23 +394,91 @@
     pl.semaphore_wait(line_sem.at[1], 2)
     greet_line(2)
 
-    for which, t in ((0, 0), (1, GROUP - 1)):
-        for i in range(NV):
-            seg1[which, i] = hg[t, i]
+    for i in range(NV):
+        seg1[0, i] = jnp.where(sub3 == 0, hg[1, i], hg[0, i])
+        seg1[1, i] = jnp.where(sub3 == GROUP - 1, hg[GROUP - 2, i], hg[GROUP - 1, i])
     tree_up_matrices(seg1, la1, fb1, keep)
 
-    def slot(which, i, column):
-        if column < 8:
-            return which * NV + i, column
-        return 2 * NV + i, which * 3 + column - 8
-
-    for i in range(NV):
-        tmp[2 * NV + i, 6:8, :] = jnp.zeros((2, 128), f32)
     for which in range(2):
         for i in range(NV):
+            dev[which, i] = jnp.zeros((2, GROUP, 128), f32)
             for c in range(2 * NV):
-                r, j = slot(which, i, c)
-                tmp[r, j : j + 1, :] = seg1[which, i, c, 0:1, :]
+                dev[which, i, c // 8, c % 8 : c % 8 + 1, :] = seg1[which, i, c, 0:1, :]
+    everywhere = lambda row: jnp.broadcast_to(row, (GROUP, 128))
+    up_a = [[everywhere(us[1, i, k, 0:1, :]) for k in range(NV)] for i in range(NV)]
+    low_z = [
+        [everywhere(ls[GROUP - 1, i, k, GROUP - 1 :, :]) for k in range(NV)] for i in range(NV)
+    ]
+    prod_a = mm(up_a, [dev[0, i] for i in range(NV)])
+    prod_z = mm(low_z, [dev[1, i] for i in range(NV)])
+    for i in range(NV):
+        part[0, i] = prod_a[i]
+        part[1, i] = prod_z[i]
+        ends[0, i] = jnp.zeros((2, GROUP, 128), f32)
+        ends[1, i] = jnp.zeros((2, GROUP, 128), f32)
+
+    for c in copies_rim:
+        c.wait()
+    rim_prev = jnp.where(line == 0, 0.0, rim_in[0])
+    rim_next = jnp.where(line == n_line - 1, 0.0, rim_in[1])
+    mean[0] = 0.25 * (rim_prev + rim_out[1])
+    mean[1] = 0.25 * (rim_next + rim_out[0])
+    for i in range(NV):
+        for k in range(NV):
+            for which in range(2):
+                q = SYM[i][k]
+                e = mean[which, q : q + 1, :]
+                e = -e if which == 0 else e
+                if i == k:
+                    e = e - 2.0 * mean[which, NSYM + NV : NSYM + NV + 1, :]
+                c = k + which * NV
+                ends[which, i, c // 8, c % 8 : c % 8 + 1, :] = e
+    for i in range(NV):
+        xst[0, i] = jnp.where(
+            first_row, rim_prev[NSYM + i : NSYM + i + 1, :], roll(xst[GROUP, i], 1, 0)
+        )
+        xst[GROUP + 1, i] = jnp.where(
+            last_row, rim_next[NSYM + i : NSYM + i + 1, :], roll(xst[1, i], GROUP - 1, 0)
+        )
+    diag_a = everywhere(
+        time_ref[0:1, :] + 2.0 * mean[0, NSYM + NV : NSYM + NV + 1, :] + fs[1, 0:1, :]
+    )
+    diag_z = everywhere(
+        time_ref[points - 1 :, :]
+        + fs[GROUP - 1, GROUP - 1 :, :]
+        + 2.0 * mean[1, NSYM + NV : NSYM + NV + 1, :]
+    )
+    column = lax.broadcasted_iota(jnp.int32, (2, GROUP, 128), 0) * GROUP
+    column = column + lax.broadcasted_iota(jnp.int32, (2, GROUP, 128), 1)
+    is_p = column < NV
+    inv_a = inverse(
+        [
+            [(diag_a if i == k else 0.0) - spread(part, (0, i), k) for k in range(NV)]
+            for i in range(NV)
+        ]
+    )
+    row_a = mm(inv_a, [jnp.where(is_p, ends[0, i], -prod_a[i]) for i in range(NV)])
+    low_elem = [[spread(part, (1, i), k) for k in range(NV)] for i in range(NV)]
+    cross = mm(low_elem, row_a)
+    for i in range(NV):
+        part[2, i] = row_a[i]
+        part[3, i] = cross[i] - prod_z[i]
+    inv_z = inverse(
+        [
+            [(diag_z if i == k else 0.0) + spread(part, (3, i), NV + k) for k in range(NV)]
+            for i in range(NV)
+        ]
+    )
+    end_z = mm(inv_z, [jnp.where(is_p, cross[i], ends[1, i]) for i in range(NV)])
+    mix = [[spread(part, (2, i), NV + k) for k in range(NV)] for i in range(NV)]
+    through = mm(mix, end_z)
+    end_a = [jnp.where(is_p, row_a[i], 0.0) - through[i] for i in range(NV)]
+    for i in range(NV):
+        for k in range(NV):
+            small[0, i, k] = inv_a[i][k]
+            small[1, i, k] = inv_z[i][k]
+        dev[0, i] = end_a[i]
+        dev[1, i] = end_z[i]
 
     pl.semaphore_wait(line_sem.at[2], 2)
     pl.semaphore_wait(plane_sem.at[1], 2)
@@ -428,6 +493,10 @@
         after = jnp.where(no_next, 0.0, span_in[1, :, rows, :])
         rhs = -0.5 * (xst[t + 2] - xst[t])
         rhs = rhs + span_weight * (after - 2.0 * state_ref[:, rows, :] + before)
+        if t == 0:
+            rhs_a = rhs
+        if t == GROUP - 1:
+            rhs_z = roll(rhs, 1, 1)
         for k in range(NV):
             rhs = rhs - ls[t, k] * d[k][None]
         d = pinv[t, 0] * rhs[0][None]
@@ -443,7 +512,33 @@
             es[t, i] = rows[i]
         e = es[t]
 
-    first, last = tree_up_rhs(es[0], es[GROUP - 1], la1, fb1, keep)
+    first, last = tree_up_rhs(
+        jnp.where(sub3 == 0, es[1], es[0]),
+        jnp.where(sub3 == GROUP - 1, es[GROUP - 2], es[GROUP - 1]),
+        la1, fb1, keep,
+    )
+
+    def apply(matrix, vector):
+        out = []
+        for i in range(NV):
+            acc = matrix(i, 0) * vector[0]
+            for k in range(1, NV):
+                acc = acc + matrix(i, k) * vector[k]
+            out.append(acc)
+        return out
+
+    first = apply(lambda i, k: everywhere(us[1, i, k, 0:1, :]), first)
+    last = apply(lambda i, k: everywhere(ls[GROUP - 1, i, k, GROUP - 1 :, :]), last)
+    part_a = apply(lambda i, k: small[0, i, k], [rhs_a[i] - first[i] for i in range(NV)])
+    carried = apply(lambda i, k: spread(part, (1, i), k), part_a)
+    value_z = apply(
+        lambda i, k: small[1, i, k], [rhs_z[i] - last[i] + carried[i] for i in range(NV)]
+    )
+    back = apply(lambda i, k: spread(part, (2, i), NV + k), value_z)
+    value_a = [part_a[i] - back[i] for i in range(NV)]
+    for which, value in ((0, value_a), (1, value_z)):
+        for i in range(NV):
+            dev[which, i, 1, 2:3, :] = value[i][0:1, :]
 
     def two_port_load(seg, landed):
         for s in range(GROUP):
@@ -456,11 +551,19 @@
             seg[0, i, 1] = packed[2 * NV + i]
             seg[1, i, 1] = roll(packed[2 * NV + i], GROUP - 3, 0)
 
-    for which, value in ((0, first), (1, last)):
-        for i in range(NV):
-            r, j = slot(which, i, 2 * NV)
-            tmp[r, j : j + 1, :] = value[i, 0:1, :]
-    packed = swap_blocks(tmp[...])
+    def pack(seg):
+        return swap_blocks(
+            jnp.concatenate(
+                [seg[0, :, 0], seg[1, :, 0]]
+                + [
+                    jnp.where(sub2 < 3, seg[0, i, 1], roll(seg[1, i, 1], 3, 0))[None]
+                    for i in range(NV)
+                ],
+                axis=0,
+            )
+        )
+
+    packed = pack(dev)
     for s in range(GROUP):
         for r in range(PACKS):
             a_out[s, r] = packed[r, s : s + 1, :]
@@ -480,16 +583,7 @@
     two_port_load(seg2, a_in)
     tree_up_lanes(seg2, near, temp, la2, fb2)
 
-    packed = swap_blocks(
-        jnp.concatenate(
-            [seg2[0, :, 0], seg2[1, :, 0]]
-            + [
-                jnp.where(sub2 < 3, seg2[0, i, 1], roll(seg2[1, i, 1], 3, 0))[None]
-                for i in range(NV)
-            ],
-            axis=0,
-        )
-    )
+    packed = pack(seg2)
     for r in range(PACKS):
         b_out[r] = packed[r, 0:1, :]
     copies = []
@@ -544,6 +638,20 @@
     packed = swap_blocks(tmp[0:2])
     p = [jnp.broadcast_to(packed[0, i : i + 1, :], (GROUP, 128)) for i in range(NV)]
     n = [jnp.broadcast_to(packed[1, i : i + 1, :], (GROUP, 128)) for i in range(NV)]
+    ends_of = []
+    for which in range(2):
+        rows = []
+        for i in range(NV):
+            terms = [spread(dev, (which, i), k) * p[k] for k in range(NV)]
+            terms += [spread(dev, (which, i), NV + k) * n[k] for k in range(NV)]
+            while len(terms) > 1:
+                terms = [
+                    terms[j] + terms[j + 1] if j + 1 < len(terms) else terms[j]
+                    for j in range(0, len(terms), 2)
+                ]
+            rows.append(spread(dev, (which, i), 2 * NV) - terms[0])
+        ends_of.append(rows)
+    p, n = ends_of
     get = lambda ref: lambda level, i, column: ref[level, i, column]
     p, n = tree_down(p, n, get(la1), get(fb1), 0, 1, sub2)
     pn = jnp.concatenate([x[None] for x in p + n], axis=0)
@@ -590,6 +698,11 @@
             pltpu.VMEM((3, nv, 2 * nv + 1) + tile, f32),
             pltpu.VMEM((3, nv, 2 * nv + 1) + tile, f32),
             pltpu.VMEM((3, 5, nv, nv) + tile, f32),
+            pltpu.VMEM((2, nv, 2) + tile, f32),
+            pltpu.VMEM((4, nv, 2) + tile, f32),
+            pltpu.VMEM((2, nv, 2) + tile, f32),
+            pltpu.VMEM((2, 24, lines), f32),
+            pltpu.VMEM((2, nv, nv) + tile, f32),
             pltpu.VMEM((2, nv, 2) + tile, f32),
             pltpu.VMEM((3, nv, 2) + tile, f32),
             pltpu.VMEM((3, nv, 2) + tile, f32),

time: 37.8 us -> 35.5 us (0.939)
  Pallas kernels: 37 us -> 34.7 us
    pallas_call x1, Pallas kernels: 37 us -> 34.7 us  [per_device(): pl.pallas_call(kernel, out_shape=pltpu.VMEM((nv, points, lines), f32), in...]
where the time goes in v3:
time: 35.5 us; the launch traced here: 35.4 us
  Pallas kernels  34.7 us (98%)
  local copies, waits for them, and re-layouts  0.67 us (2%)
    pallas_call x1, Pallas kernels, per_device(): pl.pallas_call(kernel, out_shape=pltpu.VMEM((nv, points, lines), f32), in...  34.7 us

profile of v3, /device:TPU:1, one launch (start us, length us, event | category | flops | bytes accessed | tf_op | source)
XLA Modules:
  0.0 35.4 jit_solution(15560399636861456371)
XLA Ops:
  0.0 34.7 %sweep.1 = f32[5,64,128]{2,1,0:T(8,128)S(1)} custom-call(bf16[5,5,64,128]{3,2,1,0:T(8,128)(2,1)} %bitcast.9, f32[5,64,128]{2,1,0:T(8,128)} %bitcast.10, f32[64,128]{1,0:T(8,128)} %bitcast.11, f32[64,128]{1,0:T(8,128)} %bitcast.12, f32[64,128]{1,0:T(8,128)} %bitcast.13), custom_call_target="tpu_custom_call" | custom-call | tf_op jit(solution)/shard_map/sweep/pallas_call | solution.py:671
  34.7 0.7 %copy.8 = f32[5,1,64,128]{3,2,1,0:T(8,128)} copy(f32[5,1,64,128]{3,2,1,0:T(8,128)S(1)} %bitcast.8) | data formatting | bytes 327680

commit v4 on v3

--- a/solution.py
+++ b/solution.py
@@ -226,17 +226,12 @@
     members = [plane * GROUP + lax.rem(member + o, GROUP) for o in range(1, GROUP)]
     planes = [lax.rem(plane + o, GROUP) * GROUP + member for o in range(1, GROUP)]
 
+    pairs = [(metric_hbm, metric_ref), (diss_hbm, diss_ref), (time_hbm, time_ref)]
+    pairs += [(jac_hbm.at[i], jac_ref.at[i]) for i in range(NV)]
+    pairs += [(state_hbm.at[i], state_ref.at[i]) for i in range(NV)]
     loads = [
         pltpu.make_async_copy(source, target, load_sem.at[i])
-        for i, (source, target) in enumerate(
-            (
-                (jac_hbm, jac_ref),
-                (state_hbm, state_ref),
-                (metric_hbm, metric_ref),
-                (diss_hbm, diss_ref),
-                (time_hbm, time_ref),
-            )
-        )
+        for i, (source, target) in enumerate(pairs)
     ]
     for c in loads:
         c.start()
@@ -269,46 +264,6 @@
             rim_out[side, NSYM + i : NSYM + i + 1, :] = flux_ref[i, row : row + 1, :]
         rim_out[side, NSYM + NV : NSYM + NV + 1, :] = diss_ref[row : row + 1, :]
         rim_out[side, NSYM + NV + 1 :, :] = jnp.zeros((24 - NSYM - NV - 1, 128), f32)
-
-    pl.semaphore_wait(barrier, len(peers))
-
-    def greet(sem, size, step, position, spread_by, round_at):
-        reach = (1 << round_at)
-        for other in (lax.rem(position + reach, size), lax.rem(position + size - reach, size)):
-            pl.semaphore_signal(
-                sem.at[round_at], inc=1, device_id=(other * step + spread_by, span),
-                device_id_type=MESH,
-            )
-
-    def greet_line(round_at):
-        greet(line_sem, n_line, 1, line, 0, round_at)
-
-    def greet_plane(round_at):
-        greet(plane_sem, n_line // GROUP, GROUP, plane, member, round_at)
-
-    greet_line(0)
-    greet_plane(0)
-
-    copies_rim = []
-    for side, target in ((0, line_next), (1, line_prev)):
-        copies_rim.append(
-            pltpu.make_async_remote_copy(
-                src_ref=rim_out.at[side], dst_ref=rim_in.at[side],
-                send_sem=rim_sem.at[0, side], recv_sem=rim_sem.at[1, side],
-                device_id=(target, span), device_id_type=MESH,
-            )
-        )
-        copies_rim[-1].start()
-    copies_span = []
-    for side, target in ((0, span_next), (1, span_prev)):
-        copies_span.append(
-            pltpu.make_async_remote_copy(
-                src_ref=state_hbm, dst_ref=span_in.at[side],
-                send_sem=span_sem.at[0, side], recv_sem=span_sem.at[1, side],
-                device_id=(line, target), device_id_type=MESH,
-            )
-        )
-        copies_span[-1].start()
 
     for t in range(GROUP):
         fst[t + 1] = sym_ref[:, pl.ds(t, GROUP, stride=GROUP), :]
@@ -334,6 +289,47 @@
 
     lax.fori_loop(0, GROUP + 1, faces, 0)
 
+    pl.semaphore_wait(barrier, len(peers))
+
+    def greet(sem, size, step, position, spread_by, round_at):
+        reach = (1 << round_at)
+        for other in (lax.rem(position + reach, size), lax.rem(position + size - reach, size)):
+            pl.semaphore_signal(
+                sem.at[round_at], inc=1, device_id=(other * step + spread_by, span),
+                device_id_type=MESH,
+            )
+
+    def greet_line(round_at):
+        greet(line_sem, n_line, 1, line, 0, round_at)
+
+    def greet_plane(round_at):
+        greet(plane_sem, n_line // GROUP, GROUP, plane, member, round_at)
+
+    greet_line(0)
+    greet_plane(0)
+
+    copies_rim = []
+    for side, target in ((0, line_next), (1, line_prev)):
+        copies_rim.append(
+            pltpu.make_async_remote_copy(
+                src_ref=rim_out.at[side], dst_ref=rim_in.at[side],
+                send_sem=rim_sem.at[0, side], recv_sem=rim_sem.at[1, side],
+                device_id=(target, span), device_id_type=MESH,
+            )
+        )
+        copies_rim[-1].start()
+    copies_span = []
+    for side, target in ((0, span_next), (1, span_prev)):
+        copies_span.append(
+            pltpu.make_async_remote_copy(
+                src_ref=state_hbm, dst_ref=span_in.at[side],
+                send_sem=span_sem.at[0, side], recv_sem=span_sem.at[1, side],
+                device_id=(line, target), device_id_type=MESH,
+            )
+        )
+        copies_span[-1].start()
+
+
     for t in range(GROUP):
         dst[t] = fs[t] + time_ref[pl.ds(t, GROUP, stride=GROUP), :] + fs[t + 1]
 
@@ -373,26 +369,24 @@
             wc[GROUP, i, k] = jnp.where(last_row, 0.0, wc[GROUP, i, k])
             wc[GROUP, i, NV + k] = jnp.where(last_row, -same, wc[GROUP, i, NV + k])
             pinv[GROUP - 1, k, i] = jnp.where(last_row, 0.0, pinv[GROUP - 1, k, i])
+
+    for i in range(NV):
+        hg[GROUP - 1, i] = wc[GROUP, i]
+
+    def spikes(step, carry):
+        t = GROUP - 2 - step
+        c = [[wc[t + 1, i, NV + k] for k in range(NV)] for i in range(NV)]
+        prod = mm(c, [hg[t + 1, i] for i in range(NV)])
+        for i in range(NV):
+            hg[t, i, 0:NV] = wc[t + 1, i, 0:NV] - prod[i][0:NV]
+            hg[t, i, NV:] = -prod[i][NV:]
+        return carry
+
+    lax.fori_loop(0, GROUP - 1, spikes, 0)
     pl.semaphore_wait(line_sem.at[0], 2)
     pl.semaphore_wait(plane_sem.at[0], 2)
     greet_line(1)
     greet_plane(1)
-
-    for i in range(NV):
-        hg[GROUP - 1, i] = wc[GROUP, i]
-
-    def spikes(step, carry):
-        t = GROUP - 2 - step
-        c = [[wc[t + 1, i, NV + k] for k in range(NV)] for i in range(NV)]
-        prod = mm(c, [hg[t + 1, i] for i in range(NV)])
-        for i in range(NV):
-            hg[t, i, 0:NV] = wc[t + 1, i, 0:NV] - prod[i][0:NV]
-            hg[t, i, NV:] = -prod[i][NV:]
-        return carry
-
-    lax.fori_loop(0, GROUP - 1, spikes, 0)
-    pl.semaphore_wait(line_sem.at[1], 2)
-    greet_line(2)
 
     for i in range(NV):
         seg1[0, i] = jnp.where(sub3 == 0, hg[1, i], hg[0, i])
@@ -417,6 +411,8 @@
         ends[0, i] = jnp.zeros((2, GROUP, 128), f32)
         ends[1, i] = jnp.zeros((2, GROUP, 128), f32)
 
+    pl.semaphore_wait(line_sem.at[1], 2)
+    greet_line(2)
     for c in copies_rim:
         c.wait()
     rim_prev = jnp.where(line == 0, 0.0, rim_in[0])
@@ -720,7 +716,7 @@
             pltpu.VMEM((GROUP, 2, 1, lines), f32),
             pltpu.SemaphoreType.REGULAR((3,)),
             pltpu.SemaphoreType.REGULAR((2,)),
-            pltpu.SemaphoreType.DMA((5,)),
+            pltpu.SemaphoreType.DMA((3 + 2 * NV,)),
             pltpu.SemaphoreType.DMA((2, 2)),
             pltpu.SemaphoreType.DMA((2, 2)),
             pltpu.SemaphoreType.DMA((2, GROUP)),

time: 35.5 us -> 35.6 us (level)
  no operation moved by 1% of the time
where the time goes in v4:
time: 35.6 us; the launch traced here: 35.4 us
  Pallas kernels  34.7 us (97%)
  local copies, waits for them, and re-layouts  0.67 us (2%)
    pallas_call x1, Pallas kernels, per_device(): pl.pallas_call(kernel, out_shape=pltpu.VMEM((nv, points, lines), f32), in...  34.7 us

profile of v4, /device:TPU:1, one launch (start us, length us, event | category | flops | bytes accessed | tf_op | source)
XLA Modules:
  0.0 35.4 jit_solution(11584885193676216939)
XLA Ops:
  0.0 34.7 %sweep.1 = f32[5,64,128]{2,1,0:T(8,128)S(1)} custom-call(bf16[5,5,64,128]{3,2,1,0:T(8,128)(2,1)} %bitcast.9, f32[5,64,128]{2,1,0:T(8,128)} %bitcast.10, f32[64,128]{1,0:T(8,128)} %bitcast.11, f32[64,128]{1,0:T(8,128)} %bitcast.12, f32[64,128]{1,0:T(8,128)} %bitcast.13), custom_call_target="tpu_custom_call" | custom-call | tf_op jit(solution)/shard_map/sweep/pallas_call | solution.py:667
  34.7 0.7 %copy.8 = f32[5,1,64,128]{3,2,1,0:T(8,128)} copy(f32[5,1,64,128]{3,2,1,0:T(8,128)S(1)} %bitcast.8) | data formatting | bytes 327680
